TPU v7x, 512 devices: a whole 4x4x16 slice. The times are simulated.
512 devices in a mesh: tok: 64 (over y_lo, z, core), row: 8 (over y_hi, x).
Axes of the slice: x: 4, y: 4 (y_hi: 2, y_lo: 2; y = y_hi * 2 + y_lo), z: 16, core: 2. Of those that a mesh axis runs over, the one named last changes fastest.
Arguments:
- calib: bfloat16 [8192, 4096], P('row', 'tok'), may hold values from -8 to 8
- base_weight: bfloat16 [8192, 4096], P('tok', 'row'), may hold values from -6 to 6
- keep_blocks: int32 [64, 16], replicated, may hold values from 0 to 31, all different within a row
Outputs:
- refined: bfloat16 [8192, 4096], P('tok', 'row')
Inputs may be any that keep to these rules, and one draw needn't show every extreme that they name: `keep_blocks`: each row lists 16 different block columns, and every block column is listed in some row.
All inputs are finite; a program needn't handle non-finite values.
Results may differ from a plain program's by a relative error of at most 0.0085.
Values may be sent and summed in bfloat16 or wider, within the bound.
No kernel may reach another device: no remote copies, remote signals or barrier semaphores. Data moves between devices by JAX's collectives and lax.ppermute only.
A program may use at most 64 MiB of HBM per device.

v0:
```python
import jax
import jax.numpy as jnp
from jax import lax
from jax.sharding import PartitionSpec as P

BLOCK = 128


def block_table(keep_blocks, ncols):
    labels = jnp.arange(ncols, dtype=jnp.int32)
    hits = (keep_blocks[:, :, None] == labels[None, None, :]).astype(jnp.float32)
    return jnp.sum(hits, axis=1)


def selector(first, count, nblocks):
    ids = (first + jnp.arange(count, dtype=jnp.int32)) // BLOCK
    return (ids[:, None] == jnp.arange(nblocks, dtype=jnp.int32)[None, :]).astype(jnp.float32)


def residual_product(diff, gram_cols):
    return jnp.dot(
        lax.all_gather(diff, "row", axis=1, tiled=True),
        gram_cols,
        preferred_element_type=jnp.float32,
    )


def on_device(calib, base_weight, keep_blocks):
    tok_pos = lax.axis_index("tok")
    row_pos = lax.axis_index("row")
    rows = base_weight.shape[0]
    cols = base_weight.shape[1]
    width = cols * lax.axis_size("row")
    tokens = calib.shape[0] * lax.axis_size("row")
    block_map = block_table(keep_blocks, width // BLOCK)
    row_sel = selector(tok_pos * rows, rows, block_map.shape[0])
    col_sel = selector(row_pos * cols, cols, block_map.shape[1])
    row_map = jnp.dot(row_sel, block_map)
    keep_local = jnp.dot(row_map, col_sel.T)
    base_float = base_weight.astype(jnp.float32)
    weight = (keep_local * base_float).astype(jnp.bfloat16)
    partial_value = lax.dot_general(
        calib,
        lax.all_gather(calib, "tok", axis=1, tiled=True),
        (((0,), (0,)), ((), ())),
        preferred_element_type=jnp.float32,
    )
    summed = lax.psum_scatter(partial_value, "row", scatter_dimension=1, tiled=True)
    gram_block = (summed / tokens).astype(jnp.bfloat16)
    gram_cols = lax.all_gather(gram_block, "tok", axis=0, tiled=True)
    diff = (weight.astype(jnp.float32) - base_float).astype(jnp.bfloat16)
    grad = residual_product(diff, gram_cols)
    weight = (weight.astype(jnp.float32) - 0.25 * keep_local * grad).astype(jnp.bfloat16)
    diff = (weight.astype(jnp.float32) - base_float).astype(jnp.bfloat16)
    grad = residual_product(diff, gram_cols)
    weight = (weight.astype(jnp.float32) - 0.25 * keep_local * grad).astype(jnp.bfloat16)
    return weight


def solution(mesh):
    return jax.shard_map(
        on_device,
        mesh=mesh,
        in_specs=(P("row", "tok"), P("tok", "row"), P()),
        out_specs=P("tok", "row"),
        check_vma=False,
    )
```

profile of v0, /device:TPU:2, one launch (start us, length us, event | category | flops | bytes accessed | tf_op | source)
XLA Modules:
  0.0 499.5 jit_solution(11192664810128790291)
XLA Ops:
  6.5 0.0 all-gather.7.cloned.1.call-start
  6.5 0.7 all-gather.7.cloned.1.call-update
  7.3 0.0 copy-start.1
  7.3 0.0 copy-start
  7.3 0.0 reduce-scatter.2.cloned.1.call-start
  7.3 135.7 %all-gather.7.cloned.1.call-done = bf16[1024,4096]{0,1:T(8,128)(2,1)} async-done(((bf16[1024,64]{0,1:T(8,128)(2,1)}), bf16[1024,4096]{0,1:T(8,128)(2,1)}) %all-gather.7.cloned.1.call-update) | async-done | bytes 8388624 | tf_op jit(solution)/shard_map/all_gather | solution.py:44
  143.0 7.2 %fusion.17 = f32[64,4096]{1,0:T(8,128)} fusion(bf16[1024,64]{0,1:T(8,128)(2,1)} %param.3, bf16[1024,4096]{0,1:T(8,128)(2,1)} %all-gather.7.cloned.1.call-done), kind=kOutput, calls=%fused_computation.35 | convolution fusion | flops 536870912 | bytes 9568256 | tf_op jit(solution)/shard_map/dot_general | solution.py:42
  150.2 0.0 reduce-scatter.2.cloned.1.call-update
  150.2 0.0 all-gather.5.cloned.1.call-start
  150.3 0.0 copy-done.1
  150.4 0.0 copy-done
  150.4 1.0 fusion.9
  151.4 0.0 all-gather.5.cloned.1.call-update
  151.4 0.0 all-gather.9.cloned.1.call-start
  151.5 81.9 %reduce-scatter.2.cloned.1.call-done = f32[64,512]{1,0:T(8,128)} async-done(((f32[64,4096]{1,0:T(8,128)}), f32[64,512]{1,0:T(8,128)}) %reduce-scatter.2.cloned.1.call-update) | async-done | bytes 131088 | tf_op jit(solution)/shard_map/reduce_scatter | solution.py:48
  233.3 1.5 multiply_convert_fusion
  234.9 0.0 all-gather.9.cloned.1.call-update
  234.9 0.0 all-gather.11.cloned.1.call-start
  234.9 64.8 %all-gather.5.cloned.1.call-done = bf16[128,4096]{1,0:T(8,128)(2,1)} async-done(((bf16[128,512]{1,0:T(8,128)(2,1)}), bf16[128,4096]{1,0:T(8,128)(2,1)}) %all-gather.5.cloned.1.call-update) | async-done | bytes 1048592 | tf_op jit(solution)/shard_map/all_gather | solution.py:22
  299.7 126.0 %all-gather.9.cloned.1.call-done = bf16[4096,512]{1,0:T(8,128)(2,1)} async-done(((bf16[64,512]{1,0:T(8,128)(2,1)}), bf16[4096,512]{1,0:T(8,128)(2,1)}) %all-gather.9.cloned.1.call-update) | async-done | bytes 4194320 | tf_op jit(solution)/shard_map/all_gather | solution.py:50
  425.7 3.9 fusion.10
  429.7 0.0 all-gather.11.cloned.1.call-update
  429.7 59.4 %all-gather.11.cloned.1.call-done = bf16[128,4096]{1,0:T(8,128)(2,1)} async-done(((bf16[128,512]{1,0:T(8,128)(2,1)}), bf16[128,4096]{1,0:T(8,128)(2,1)}) %all-gather.11.cloned.1.call-update) | async-done | bytes 1048592 | tf_op jit(solution)/shard_map/all_gather | solution.py:22
  489.1 3.9 fusion.4
  (3 shorter events, 0.1 us)
Async XLA Ops:
  6.5 136.5 %all-gather.7.cloned.1.call-start = ((), (), s32[]{:S(2)}) async-start(), calls=%async_computation.2 | async-start | bytes 8519680 | tf_op jit(solution)/shard_map/all_gather | solution.py:44
  7.3 143.1 %copy-start.1 = (s32[64,16]{0,1:T(8,128)S(1)}, s32[64,16]{0,1:T(8,128)}, u32[]{:S(2)}) copy-start(s32[64,16]{0,1:T(8,128)} %param.5) | copy-start | bytes 12292
  7.3 143.1 %copy-start = (bf16[128,512]{1,0:T(8,128)(2,1)S(1)}, bf16[128,512]{1,0:T(8,128)(2,1)}, u32[]{:S(2)}) copy-start(bf16[128,512]{1,0:T(8,128)(2,1)} %param.4) | copy-start | bytes 393220
  7.3 226.0 %reduce-scatter.2.cloned.1.call-start = ((), (), s32[]{:S(2)}) async-start(), calls=%async_computation.3 | async-start | bytes 1179648 | tf_op jit(solution)/shard_map/reduce_scatter | solution.py:48
  150.2 149.5 %all-gather.5.cloned.1.call-start = ((), (), s32[]{:S(2)}) async-start(), calls=%async_computation.1 | async-start | bytes 1179648 | tf_op jit(solution)/shard_map/all_gather | solution.py:22
  151.4 274.3 %all-gather.9.cloned.1.call-start = ((), (), s32[]{:S(2)}) async-start(), calls=%async_computation.4 | async-start | bytes 4259840 | tf_op jit(solution)/shard_map/all_gather | solution.py:50
  234.9 254.2 %all-gather.11.cloned.1.call-start = ((), (), s32[]{:S(2)}) async-start(), calls=%async_computation.5 | async-start | bytes 1179648 | tf_op jit(solution)/shard_map/all_gather | solution.py:22
Sparse Core Ops, SparseCore 0:
  9.5 133.4 all-gather.6
  150.3 82.9 reduce-scatter.1
  236.8 62.8 all-gather.4
  301.9 123.7 all-gather.8
  429.8 59.2 all-gather.10
where the time goes:
time: 500 us
  waiting for transfers between devices  469 us (94%)
  matrix products  16 us (3%)
  between operations  13.2 us (3%)
    all_gather x1, waiting for transfers between devices, on_device(): lax.all_gather(calib, 'tok', axis=1, tiled=True)  136 us
    all_gather x1, waiting for transfers between devices, on_device(): gram_cols = lax.all_gather(gram_block, 'tok', axis=0, tiled=True)  126 us
    all_gather x2, waiting for transfers between devices, residual_product(): lax.all_gather(diff, 'row', axis=1, tiled=True)  124 us
    reduce_scatter x1, waiting for transfers between devices, on_device(): lax.psum_scatter(partial_value, 'row', scatter_dimension=1, tiled=True)  81.9 us
  transfers between devices with their start and end apart: 5, of which 5 were waited for; matrix products, arithmetic and copies ran while one was open for 1% of the time, Pallas kernels for 0%

commit v1 on v0

--- a/solution.py
+++ b/solution.py
@@ -19,7 +19,9 @@
 
 def residual_product(diff, gram_cols):
     return jnp.dot(
-        lax.all_gather(diff, "row", axis=1, tiled=True),
+        jnp.concatenate(
+            lax.all_to_all(jnp.stack([diff] * lax.axis_size("row")), "row", 0, 0), axis=1
+        ),
         gram_cols,
         preferred_element_type=jnp.float32,
     )

time: 500 us -> 398 us (0.80)
  the two profiles are of different devices: /device:TPU:2 before, /device:TPU:1 now
where the time goes in v1:
time: 398 us
  waiting for transfers between devices  326 us (82%)
  blocking collectives  41.9 us (11%)
  matrix products  14.2 us (4%)
  between operations  13.2 us (3%)
    all_gather x1, waiting for transfers between devices, on_device(): lax.all_gather(calib, 'tok', axis=1, tiled=True)  137 us
    all_gather x1, waiting for transfers between devices, on_device(): gram_cols = lax.all_gather(gram_block, 'tok', axis=0, tiled=True)  107 us
    reduce_scatter x1, waiting for transfers between devices, on_device(): lax.psum_scatter(partial_value, 'row', scatter_dimension=1, tiled=True)  81.3 us
    all_to_all x2, blocking collectives, residual_product(): lax.all_to_all(jnp.stack([diff] * lax.axis_size('row')), 'row', 0, 0)  41.9 us
  transfers between devices with their start and end apart: 3, of which 3 were waited for; matrix products, arithmetic and copies ran while one was open for 0% of the time, Pallas kernels for 0%

profile of v1, /device:TPU:1, one launch (start us, length us, event | category | flops | bytes accessed | tf_op | source)
XLA Modules:
  0.0 397.8 jit_solution(9340456343952404879)
XLA Ops:
  6.5 0.0 all-gather.3.cloned.1.call-start
  6.5 0.7 all-gather.3.cloned.1.call-update
  7.3 0.0 copy-start.1
  7.3 0.0 copy-start
  7.3 0.0 reduce-scatter.2.cloned.1.call-start
  7.3 136.8 %all-gather.3.cloned.1.call-done = bf16[1024,4096]{0,1:T(8,128)(2,1)} async-done(((bf16[1024,64]{0,1:T(8,128)(2,1)}), bf16[1024,4096]{0,1:T(8,128)(2,1)}) %all-gather.3.cloned.1.call-update) | async-done | bytes 8388624 | tf_op jit(solution)/shard_map/all_gather | solution.py:46
  144.1 7.2 %fusion.17 = f32[64,4096]{1,0:T(8,128)} fusion(bf16[1024,64]{0,1:T(8,128)(2,1)} %param.3, bf16[1024,4096]{0,1:T(8,128)(2,1)} %all-gather.3.cloned.1.call-done), kind=kOutput, calls=%fused_computation.35 | convolution fusion | flops 536870912 | bytes 9568256 | tf_op jit(solution)/shard_map/dot_general | solution.py:44
  151.3 0.0 reduce-scatter.2.cloned.1.call-update
  151.3 0.0 all-gather.5.cloned.1.call-start
  151.3 81.3 %reduce-scatter.2.cloned.1.call-done = f32[64,512]{1,0:T(8,128)} async-done(((f32[64,4096]{1,0:T(8,128)}), f32[64,512]{1,0:T(8,128)}) %reduce-scatter.2.cloned.1.call-update) | async-done | bytes 131088 | tf_op jit(solution)/shard_map/reduce_scatter | solution.py:50
  232.6 1.5 multiply_convert_fusion
  234.1 0.0 all-gather.5.cloned.1.call-update
  234.2 0.0 copy-done.1
  234.3 0.0 copy-done
  234.3 0.5 fusion.9
  234.7 0.1 copy.8
  234.9 0.1 stack.4
  235.0 18.6 %all_to_all.10 = bf16[8,128,512]{1,2,0:T(8,128)(2,1)S(1)} all-to-all(bf16[8,128,512]{1,2,0:T(8,128)(2,1)S(1)} %stack.4), channel_id=1, replica_groups=mesh['tok'=64,'row'=8] {'row'}, dimensions={0} | all-to-all | bytes 2097152 | tf_op jit(solution)/shard_map/all_to_all | solution.py:23
  253.6 107.5 %all-gather.5.cloned.1.call-done = bf16[4096,512]{1,0:T(8,128)(2,1)} async-done(((bf16[64,512]{1,0:T(8,128)(2,1)}), bf16[4096,512]{1,0:T(8,128)(2,1)}) %all-gather.5.cloned.1.call-update) | async-done | bytes 4194320 | tf_op jit(solution)/shard_map/all_gather | solution.py:52
  361.1 2.9 fusion.10
  364.0 0.1 copy.9
  364.2 0.1 stack.5
  364.3 23.3 %all_to_all.11 = bf16[8,128,512]{1,2,0:T(8,128)(2,1)S(1)} all-to-all(bf16[8,128,512]{1,2,0:T(8,128)(2,1)S(1)} %stack.5), channel_id=1, replica_groups=mesh['tok'=64,'row'=8] {'row'}, dimensions={0} | all-to-all | bytes 2097152 | tf_op jit(solution)/shard_map/all_to_all | solution.py:23
  387.6 3.6 fusion.4
  (3 shorter events, 0.1 us)
Async XLA Ops:
  6.5 137.6 %all-gather.3.cloned.1.call-start = ((), (), s32[]{:S(2)}) async-start(), calls=%async_computation.3 | async-start | bytes 8519680 | tf_op jit(solution)/shard_map/all_gather | solution.py:46
  7.3 227.0 %copy-start.1 = (s32[64,16]{0,1:T(8,128)S(1)}, s32[64,16]{0,1:T(8,128)}, u32[]{:S(2)}) copy-start(s32[64,16]{0,1:T(8,128)} %param.5) | copy-start | bytes 12292
  7.3 227.0 %copy-start = (bf16[128,512]{1,0:T(8,128)(2,1)S(1)}, bf16[128,512]{1,0:T(8,128)(2,1)}, u32[]{:S(2)}) copy-start(bf16[128,512]{1,0:T(8,128)(2,1)} %param.4) | copy-start | bytes 393220
  7.3 225.3 %reduce-scatter.2.cloned.1.call-start = ((), (), s32[]{:S(2)}) async-start(), calls=%async_computation.4 | async-start | bytes 1179648 | tf_op jit(solution)/shard_map/reduce_scatter | solution.py:50
  151.3 209.8 %all-gather.5.cloned.1.call-start = ((), (), s32[]{:S(2)}) async-start(), calls=%async_computation.5 | async-start | bytes 4259840 | tf_op jit(solution)/shard_map/all_gather | solution.py:52
Sparse Core Ops, SparseCore 0:
  9.5 134.5 all-gather.2
  151.4 81.1 reduce-scatter.1
  235.0 126.0 all-gather.4
